TPU v7x, 512 devices: a whole 4x8x8 slice. The times are simulated.
512 devices in a mesh: seq: 32 (over y, x), doc: 16 (over z, core).
Axes of the slice: x: 4, y: 8, z: 8, core: 2. Of those that a mesh axis runs over, the one named last changes fastest.
Arguments:
- teacher: bfloat16 [16, 4096, 4096], P('doc', 'seq'), may hold values from -24 to 24
- student: bfloat16 [16, 4096, 3072], P('doc', 'seq'), may hold values from -6 to 6
- adapter: bfloat16 [4096, 128], P(('seq', 'doc')), may hold values from -0.09375 to 0.09375
- up_weight: bfloat16 [128, 3072], replicated, may hold values from -0.53033009 to 0.53033009
- band_start: int32 [16, 4096], P('doc', 'seq'), may hold values from 0 to 4095, as said below
- band_len: int32 [16, 4096], P('doc', 'seq'), may hold values from 1 to 64, as said below
Outputs:
- student_grad: bfloat16 [16, 4096, 3072], P('doc', 'seq')
- adapter_grad: float32 [4096, 128], P(('seq', 'doc'))
- up_grad: float32 [128, 3072], P(None, 'doc')
- loss: float32 [], replicated
Inputs may be any that keep to these rules, and one draw needn't show every extreme that they name: For student token i the band lies inside the document and inside teacher rows 128 * (i // 128) - 64 to 128 * (i // 128 + 1) + 128 // 2 - 1; band_start + band_len <= 4096; the last student token of every document has the single band row 4095. `band_len`: some token of every document has a band of exactly 64 rows.
All inputs are finite; a program needn't handle non-finite values.
Results may differ from a plain program's by a relative error of at most 0.0083.
The roundings to bfloat16 on the way count: a program that leaves them out, or rounds other values in their place, can miss the bound.
Values may be sent and summed in bfloat16 or wider, within the bound.
A program may use at most 64 MiB of HBM per device.

v0:
```python
import jax
import jax.numpy as jnp
from jax import lax
from jax.sharding import Mesh
from jax.sharding import PartitionSpec as P

SEQ = ("seq_0", "seq_1")
SEQ_DOC = ("seq_0", "seq_1", "doc_0", "doc_1")
DOC = ("doc_0", "doc_1")


def from_everyone(x, axis):
    copies = jnp.broadcast_to(x, (lax.axis_size(axis), *x.shape))
    return lax.all_to_all(copies, axis, split_axis=0, concat_axis=0, tiled=True)


def in_order(pieces, dim):
    dims = list(pieces.shape[1:])
    dims[dim] *= pieces.shape[0]
    return jnp.moveaxis(pieces, 0, dim).reshape(dims)


def gather_axes(x, axes, dim):
    far, near = axes
    leading = from_everyone(x, far)
    pieces = jnp.swapaxes(from_everyone(leading, near), 0, 1)
    return in_order(pieces.reshape(-1, *x.shape), dim)


def with_halo(cells, sides, width):
    for axis, dim in sides:
        count = lax.axis_size(axis)
        ends = count - 1
        head = lax.slice_in_dim(cells, 0, width, axis=dim)
        tail = lax.slice_in_dim(cells, cells.shape[dim] - width, cells.shape[dim], axis=dim)
        cells = jnp.concatenate(
            [
                lax.ppermute(tail, axis, [(i, (i + 1) % count) for i in range(ends)]),
                cells,
                lax.ppermute(head, axis, [((i + 1) % count, i) for i in range(ends)]),
            ],
            axis=dim,
        )
    return cells


def cut_along(x, dim, devices):
    dims = x.shape
    pieces = x.reshape(*dims[:dim], devices, dims[dim] // devices, *dims[dim + 1 :])
    return jnp.moveaxis(pieces, dim, 0)


def summed_on_arrival(x, axis, dim):
    pieces = cut_along(x, dim, lax.axis_size(axis))
    arrived = lax.all_to_all(pieces, axis, split_axis=0, concat_axis=0, tiled=True)
    return arrived.sum(axis=0)


def sum_in_two_steps(x, axes, dim):
    far, near = axes
    pieces = cut_along(x, dim, lax.axis_size(far))
    nearer = summed_on_arrival(pieces, near, dim + 1)
    arrived = lax.all_to_all(nearer, far, split_axis=0, concat_axis=0, tiled=True)
    return arrived.sum(axis=0)


def filled_up(lines, devices):
    spare = -lines.shape[0] % devices
    if not spare:
        return lines
    return jnp.concatenate([lines, jnp.zeros((spare, *lines.shape[1:]), lines.dtype)])


def sum_by_parts(x, axes):
    own = sum_in_two_steps(filled_up(x, lax.axis_size(axes[0]) * lax.axis_size(axes[1])), axes, 0)
    whole = gather_axes(own, axes, 0)
    return whole[: len(x)].reshape(x.shape)


def together(arrays, axis):
    flat, at, outs = (jnp.concatenate([a.reshape(-1) for a in arrays]), 0, [])
    running = sum_by_parts(flat, axis)
    for a in arrays:
        outs.append(running[at : at + a.size].reshape(a.shape))
        at += a.size
    return tuple(outs)


def contract_rows(left, right):
    return lax.dot_general(
        left, right, (((0,), (0,)), ((), ())), preferred_element_type=jnp.float32
    )


def contract_cols(left, right):
    return lax.dot_general(
        left, right, (((1,), (1,)), ((), ())), preferred_element_type=jnp.float32
    )


def band_pass(student_rows, key_rows, firsts, lengths, up_weight, row_first):
    scale = student_rows.shape[1] ** (-0.5)
    query = contract_cols(student_rows, up_weight).astype(jnp.bfloat16)
    scores = contract_cols(query, key_rows) * scale
    position = row_first + jnp.arange(key_rows.shape[0], dtype=jnp.int32)
    inside = (position[None, :] >= firsts[:, None]) & (
        position[None, :] < (firsts + lengths)[:, None]
    )
    scores = jnp.where(inside, scores, -1e30)
    row_max = jnp.max(scores, axis=1, keepdims=True)
    weights = jnp.where(inside, jnp.exp(scores - row_max), 0.0)
    prob = weights / jnp.sum(weights, axis=1, keepdims=True)
    prob_b = prob.astype(jnp.bfloat16)
    context = jnp.dot(prob_b, key_rows, preferred_element_type=jnp.float32).astype(jnp.bfloat16)
    output = jnp.dot(context, up_weight, preferred_element_type=jnp.float32)
    residual = student_rows.astype(jnp.float32) - output
    loss_part = 0.5 * jnp.sum(residual * residual)
    out_grad = (-residual).astype(jnp.bfloat16)
    ctx_grad = contract_cols(out_grad, up_weight).astype(jnp.bfloat16)
    prob_grad = contract_cols(ctx_grad, key_rows)
    centred = prob_grad - jnp.sum(prob * prob_grad, axis=1, keepdims=True)
    score_grad = (prob * centred * scale).astype(jnp.bfloat16)
    key_grad = (contract_rows(prob_b, ctx_grad) + contract_rows(score_grad, query)).astype(
        jnp.bfloat16
    )
    query_grad = jnp.dot(score_grad, key_rows, preferred_element_type=jnp.float32).astype(
        jnp.bfloat16
    )
    up_part = contract_rows(context, out_grad) + contract_rows(query_grad, student_rows)
    student_grad = (
        residual + jnp.dot(query_grad, up_weight, preferred_element_type=jnp.float32)
    ).astype(jnp.bfloat16)
    return (student_grad, key_grad, up_part, loss_part)


def on_device(teacher, student, adapter, up_weight, band_start, band_len):
    tok_rows = teacher.shape[1]
    half_rows = tok_rows // 2
    own_rows = teacher[0]
    row_first = lax.axis_index(SEQ) * tok_rows - half_rows
    source_rows = with_halo(own_rows, ((SEQ, 0),), half_rows)
    columns = source_rows
    mapped = jnp.dot(
        columns,
        gather_axes(adapter, ("seq_0", ("seq_1", "doc_0", "doc_1")), 0),
        preferred_element_type=jnp.float32,
    )
    mapped_rows = mapped.astype(jnp.bfloat16)
    student_grad, key_grad, up_part, loss_part = band_pass(
        student[0], mapped_rows, band_start[0], band_len[0], up_weight, row_first
    )
    seq_count = lax.axis_size(SEQ)
    doc_count = lax.axis_size(DOC)
    student_width = student.shape[2]
    grad_scale = (seq_count * doc_count * tok_rows) ** (-0.5)
    columns = source_rows
    adapter_grad = (
        sum_in_two_steps(
            contract_rows(columns, key_grad), ("seq_0", ("seq_1", "doc_0", "doc_1")), 0
        )
        * grad_scale
    )
    up_total, loss_total = together((up_part, loss_part), ("seq_0", ("seq_1", "doc_0", "doc_1")))
    slice_width = student_width // doc_count
    up_grad = (
        lax.dynamic_slice_in_dim(up_total, lax.axis_index(DOC) * slice_width, slice_width, 1)
        * grad_scale
    )
    loss = loss_total / (seq_count * doc_count * tok_rows * student_width)
    return (student_grad[None], adapter_grad, up_grad, loss)


def solution(mesh):
    torus = Mesh(mesh.devices.reshape(8, 4, 8, 2), ("seq_0", "seq_1", "doc_0", "doc_1"))
    placed = (P(DOC, SEQ, None), P(DOC, SEQ, None), P(SEQ_DOC, None), P(), P(DOC, SEQ), P(DOC, SEQ))
    return jax.shard_map(
        on_device,
        mesh=torus,
        in_specs=placed,
        out_specs=(P(DOC, SEQ, None), P(SEQ_DOC, None), P(None, DOC), P()),
        check_vma=False,
    )
```

profile of v0, /device:TPU:1, one launch (start us, length us, event | category | flops | bytes accessed | tf_op | source)
XLA Modules:
  0.0 306.7 jit_solution(8302934380908617509)
XLA Ops:
  0.6 0.0 copy-start
  0.6 0.8 broadcast_in_dim.31
  1.4 14.0 %all_to_all.48 = bf16[8,8,128]{2,1,0:T(8,128)(2,1)S(1)} all-to-all(bf16[8,8,128]{2,1,0:T(8,128)(2,1)S(1)} %broadcast_in_dim.31), channel_id=1, replica_groups=mesh['seq_0'=8,'seq_1'=4,'doc_0'=8,'doc_1'=2] {'seq_0'}, dimensions={0} | all-to-all | bytes 32768 | tf_op jit(solution)/shard_map/all_to_all | solution.py:14
  15.5 1.2 broadcast_in_dim.32
  16.7 15.6 %all-to-all-start.1 = ((bf16[64,8,8,128]{3,2,1,0:T(8,128)(2,1)}), bf16[64,8,8,128]{3,2,1,0:T(8,128)(2,1)S(1)}, u32[]{:S(2)}, u32[]{:S(2)}) async-start(bf16[64,8,8,128]{3,2,1,0:T(8,128)(2,1)} %broadcast_in_dim.32), calls=%async_computation.1 | async-start | bytes 2097152 | tf_op jit(solution)/shard_map/all_to_all | solution.py:14
  32.3 2.1 slice_bitcast_fusion.1
  34.3 4.1 %collective-permute-start = (bf16[64,4096]{1,0:T(8,128)(2,1)}, bf16[64,4096]{1,0:T(8,128)(2,1)}, u32[]{:S(2)}, u32[]{:S(2)}) collective-permute-start(bf16[64,4096]{1,0:T(8,128)(2,1)} %get-tuple-element.20), channel_id=1, source_target_pairs={{0,16},{16,32},{32,48},{48,64},{64,80},{80,96},{96,112},{112,128},... | collective-permute-start | bytes 1572872 | tf_op jit(solution)/shard_map/ppermute | solution.py:38
  38.4 1.3 collective-permute-start.1
  39.7 0.0 copy-done.5
  39.7 0.0 copy-done.6
  39.8 0.0 copy-done
  39.8 0.0 copy-done.1
  39.8 0.4 convolution_convert_fusion.2
  40.1 0.0 copy-start.4
  40.2 20.6 %all-to-all-done.1 = bf16[64,8,8,128]{3,2,1,0:T(8,128)(2,1)S(1)} async-done(((bf16[64,8,8,128]{3,2,1,0:T(8,128)(2,1)}), bf16[64,8,8,128]{3,2,1,0:T(8,128)(2,1)S(1)}, u32[]{:S(2)}, u32[]{:S(2)}) %all-to-all-start.1) | async-done | bytes 1048608 | tf_op jit(solution)/shard_map/all_to_all | solution.py:14
  60.8 0.2 copy.20
  61.0 0.0 collective-permute-done
  61.0 0.0 collective-permute-done.1
  61.0 1.0 copy-done.2
  62.0 1.9 convolution_convert_fusion
  63.9 0.3 fusion.16
  64.2 0.2 fusion.10
  64.4 0.1 fusion.9
  64.6 0.1 convolution_convert_fusion.4
  64.7 1.2 multiply_reduce_fusion
  65.9 0.4 convolution_convert_fusion.1
  66.3 0.4 fusion.8
  66.6 0.3 multiply_reduce_fusion.1
  66.9 0.2 multiply_convert_fusion
  67.1 0.1 convolution_convert_fusion.3
  67.2 0.4 fusion.2
  67.6 1.4 copy.26
  69.7 13.9 %concatenate.7 = f32[393728]{0:T(1024)} concatenate(f32[393216]{0:T(1024)} %bitcast.55, f32[1]{0:T(128)} %bitcast.11, f32[511]{0:T(512)S(1)} %broadcast_in_dim.36), dimensions={0} | concatenate | bytes 3149824 | tf_op jit(solution)/shard_map/concatenate | solution.py:71
  83.7 4.2 %reshape_reshape.14 = f32[8,64,769]{2,1,0:T(8,128)} reshape(f32[393728]{0:T(1024)} %concatenate.7) | data formatting | bytes 3149824 | tf_op jit(solution)/shard_map/reshape;reshape | solution.py:49
  87.9 3.8 %copy.22 = f32[64,8,769]{2,1,0:T(8,128)} copy(f32[64,8,769]{2,0,1:T(8,128)} %bitcast.54) | data formatting | bytes 3149824 | tf_op jit(solution)/shard_map/transpose | solution.py:50
  91.7 9.7 %all-to-all-start.4 = ((f32[64,8,769]{2,1,0:T(8,128)}), f32[64,8,769]{2,1,0:T(8,128)}, u32[]{:S(2)}, u32[]{:S(2)}) async-start(f32[64,8,769]{2,1,0:T(8,128)} %copy.22), calls=%async_computation.4 | async-start | bytes 3670016 | tf_op jit(solution)/shard_map/all_to_all | solution.py:55
  101.4 0.9 fusion.11
  102.2 44.5 %all-to-all-done.4 = f32[64,8,769]{2,1,0:T(8,128)} async-done(((f32[64,8,769]{2,1,0:T(8,128)}), f32[64,8,769]{2,1,0:T(8,128)}, u32[]{:S(2)}, u32[]{:S(2)}) %all-to-all-start.4) | async-done | bytes 1574944 | tf_op jit(solution)/shard_map/all_to_all | solution.py:55
  146.7 1.6 reduce_sum.68
  148.3 0.6 all_to_all.35
  149.0 3.3 %all-to-all-start.5 = ((f32[8,1,769]{2,1,0:T(1,128)}), f32[8,1,769]{2,1,0:T(1,128)S(1)}, u32[]{:S(2)}, u32[]{:S(2)}) async-start(f32[8,1,769]{2,1,0:T(1,128)} %all_to_all.35), calls=%async_computation.5 | async-start | bytes 57344 | tf_op jit(solution)/shard_map/all_to_all | solution.py:63
  152.3 3.5 %fusion.5 = f32[4096,128]{1,0:T(8,128)} fusion(f32[256,128]{1,0:T(8,128)} %fusion.11, bf16[128,256]{1,0:T(8,128)(2,1)S(1)} %multiply_convert_fusion, bf16[128,128]{1,0:T(8,128)(2,1)} %copy-done.4, bf16[64,4096]{1,0:T(8,128)(2,1)} %collective-permute-done.1, bf16[128,4096]{1,0:T(8,128)(2,1)S(1)} %bitcast.58, bf16[64,4096]{1,0:T(8,128)(2,1)} %collective-permute-done), kind=kOutput, calls=%fused_computation.15 | convolution fusion | flops 283181056 | bytes 4423680 | tf_op jit(solution)/shard_map/dot_general | solution.py:90
  155.8 3.2 %copy.29 = f32[8,64,8,128]{3,2,0,1:T(8,128)} copy(f32[8,64,8,128]{3,2,1,0:T(8,128)} %bitcast.56) | data formatting | bytes 4194304 | tf_op jit(solution)/shard_map/reshape;reshape | solution.py:49
  159.0 0.1 all-to-all-done.5
  159.0 7.3 %all-to-all-start.2 = ((f32[64,8,8,128]{3,2,1,0:T(8,128)}), f32[64,8,8,128]{3,2,1,0:T(8,128)}, u32[]{:S(2)}, u32[]{:S(2)}) async-start(f32[64,8,8,128]{3,2,1,0:T(8,128)} %bitcast.53), calls=%async_computation.2 | async-start | bytes 4194304 | tf_op jit(solution)/shard_map/all_to_all | solution.py:55
  166.4 51.1 %all-to-all-done.2 = f32[64,8,8,128]{3,2,1,0:T(8,128)} async-done(((f32[64,8,8,128]{3,2,1,0:T(8,128)}), f32[64,8,8,128]{3,2,1,0:T(8,128)}, u32[]{:S(2)}, u32[]{:S(2)}) %all-to-all-start.2) | async-done | bytes 2097184 | tf_op jit(solution)/shard_map/all_to_all | solution.py:55
  217.5 0.6 broadcast_in_dim.37
  218.1 5.6 %all-to-all-start.6 = ((f32[8,1,769]{2,1,0:T(1,128)}), f32[8,1,769]{2,1,0:T(1,128)S(1)}, u32[]{:S(2)}, u32[]{:S(2)}) async-start(f32[8,1,769]{2,1,0:T(1,128)} %broadcast_in_dim.37), calls=%async_computation.6 | async-start | bytes 57344 | tf_op jit(solution)/shard_map/all_to_all | solution.py:14
  223.7 2.3 reduce_sum.65
  226.1 4.6 %all-to-all-done.6 = f32[8,1,769]{2,1,0:T(1,128)S(1)} async-done(((f32[8,1,769]{2,1,0:T(1,128)}), f32[8,1,769]{2,1,0:T(1,128)S(1)}, u32[]{:S(2)}, u32[]{:S(2)}) %all-to-all-start.6) | async-done | bytes 24640 | tf_op jit(solution)/shard_map/all_to_all | solution.py:14
  230.7 3.3 %all-to-all-start.3 = ((f32[8,8,128]{2,1,0:T(8,128)}), f32[8,8,128]{2,1,0:T(8,128)S(1)}, u32[]{:S(2)}, u32[]{:S(2)}) async-start(f32[8,8,128]{2,1,0:T(8,128)} %reduce_sum.65), calls=%async_computation.3 | async-start | bytes 65536 | tf_op jit(solution)/shard_map/all_to_all | solution.py:63
  234.0 6.8 %all-to-all-done.3 = f32[8,8,128]{2,1,0:T(8,128)S(1)} async-done(((f32[8,8,128]{2,1,0:T(8,128)}), f32[8,8,128]{2,1,0:T(8,128)S(1)}, u32[]{:S(2)}, u32[]{:S(2)}) %all-to-all-start.3) | async-done | bytes 32800 | tf_op jit(solution)/shard_map/all_to_all | solution.py:63
  240.8 1.4 broadcast_in_dim.38
  242.2 8.7 %all-to-all-start.7 = ((f32[64,8,769]{2,1,0:T(8,128)}), f32[64,8,769]{2,1,0:T(8,128)}, u32[]{:S(2)}, u32[]{:S(2)}) async-start(f32[64,8,769]{2,1,0:T(8,128)} %broadcast_in_dim.38), calls=%async_computation.7 | async-start | bytes 3670016 | tf_op jit(solution)/shard_map/all_to_all | solution.py:14
  250.8 1.2 fusion.1
  252.1 0.6 broadcast_multiply_fusion
  252.7 43.5 %all-to-all-done.7 = f32[64,8,769]{2,1,0:T(8,128)} async-done(((f32[64,8,769]{2,1,0:T(8,128)}), f32[64,8,769]{2,1,0:T(8,128)}, u32[]{:S(2)}, u32[]{:S(2)}) %all-to-all-start.7) | async-done | bytes 1574944 | tf_op jit(solution)/shard_map/all_to_all | solution.py:14
  296.2 1.9 copy.23
  298.0 2.3 reshape_reshape.15
  300.3 1.3 slice.28
  301.7 0.1 slice-done
  301.8 1.4 reshape.47
  303.1 1.0 dynamic-slice_multiply_fusion
  304.2 0.7 copy.24
  (14 shorter events, 0.1 us)
Async XLA Ops:
  0.6 39.1 %copy-start = (bf16[128,3072]{1,0:T(8,128)(2,1)S(1)}, bf16[128,3072]{1,0:T(8,128)(2,1)}, u32[]{:S(2)}) copy-start(bf16[128,3072]{1,0:T(8,128)(2,1)} %param.9) | copy-start | bytes 2359300
  16.7 23.0 %copy-start.5 = (s32[1,128]{1,0:T(1,128)S(1)}, s32[1,128]{1,0:T(1,128)}, u32[]{:S(2)}) copy-start(s32[1,128]{1,0:T(1,128)} %param.10) | copy-start | bytes 1540
  16.7 23.0 %copy-start.6 = (s32[1,128]{1,0:T(1,128)S(1)}, s32[1,128]{1,0:T(1,128)}, u32[]{:S(2)}) copy-start(s32[1,128]{1,0:T(1,128)} %param.11) | copy-start | bytes 1540
  16.7 23.1 %copy-start.1 = (bf16[1,128,3072]{2,1,0:T(8,128)(2,1)S(1)}, bf16[1,128,3072]{2,1,0:T(8,128)(2,1)}, u32[]{:S(2)}) copy-start(bf16[1,128,3072]{2,1,0:T(8,128)(2,1)} %param.7) | copy-start | bytes 2359300
  16.7 44.1 %all-to-all-start.1 = ((bf16[64,8,8,128]{3,2,1,0:T(8,128)(2,1)}), bf16[64,8,8,128]{3,2,1,0:T(8,128)(2,1)S(1)}, u32[]{:S(2)}, u32[]{:S(2)}) async-start(bf16[64,8,8,128]{3,2,1,0:T(8,128)(2,1)} %broadcast_in_dim.32), calls=%async_computation.1 | async-start | bytes 2097152 | tf_op jit(solution)/shard_map/all_to_all | solution.py:14
  34.3 26.6 %collective-permute-start = (bf16[64,4096]{1,0:T(8,128)(2,1)}, bf16[64,4096]{1,0:T(8,128)(2,1)}, u32[]{:S(2)}, u32[]{:S(2)}) collective-permute-start(bf16[64,4096]{1,0:T(8,128)(2,1)} %get-tuple-element.20), channel_id=1, source_target_pairs={{0,16},{16,32},{32,48},{48,64},{64,80},{80,96},{96,112},{112,128},... | collective-permute-start | bytes 1572872 | tf_op jit(solution)/shard_map/ppermute | solution.py:38
  38.4 22.6 %collective-permute-start.1 = (bf16[64,4096]{1,0:T(8,128)(2,1)S(1)}, bf16[64,4096]{1,0:T(8,128)(2,1)}, u32[]{:S(2)}, u32[]{:S(2)}) collective-permute-start(bf16[64,4096]{1,0:T(8,128)(2,1)S(1)} %get-tuple-element.21), channel_id=1, source_target_pairs={{16,0},{32,16},{48,32},{64,48},{80,64},{96,80},{112,96},{128,112},... | collective-permute-start | bytes 1572872 | tf_op jit(solution)/shard_map/ppermute | solution.py:40
  40.1 23.8 %copy-start.4 = (bf16[128,128]{1,0:T(8,128)(2,1)}, bf16[128,128]{1,0:T(8,128)(2,1)S(1)}, u32[]{:S(2)}) copy-start(bf16[128,128]{1,0:T(8,128)(2,1)S(1)} %convolution_convert_fusion.2) | copy-start | bytes 98308
  60.8 1.2 copy-start.2
  91.7 55.0 %all-to-all-start.4 = ((f32[64,8,769]{2,1,0:T(8,128)}), f32[64,8,769]{2,1,0:T(8,128)}, u32[]{:S(2)}, u32[]{:S(2)}) async-start(f32[64,8,769]{2,1,0:T(8,128)} %copy.22), calls=%async_computation.4 | async-start | bytes 3670016 | tf_op jit(solution)/shard_map/all_to_all | solution.py:55
  102.2 50.0 %copy-start.3 = (bf16[1,128,4096]{2,1,0:T(8,128)(2,1)S(1)}, bf16[1,128,4096]{2,1,0:T(8,128)(2,1)}, u32[]{:S(2)}) copy-start(bf16[1,128,4096]{2,1,0:T(8,128)(2,1)} %param.6) | copy-start | bytes 3145732
  149.0 10.1 %all-to-all-start.5 = ((f32[8,1,769]{2,1,0:T(1,128)}), f32[8,1,769]{2,1,0:T(1,128)S(1)}, u32[]{:S(2)}, u32[]{:S(2)}) async-start(f32[8,1,769]{2,1,0:T(1,128)} %all_to_all.35), calls=%async_computation.5 | async-start | bytes 57344 | tf_op jit(solution)/shard_map/all_to_all | solution.py:63
  159.0 58.5 %all-to-all-start.2 = ((f32[64,8,8,128]{3,2,1,0:T(8,128)}), f32[64,8,8,128]{3,2,1,0:T(8,128)}, u32[]{:S(2)}, u32[]{:S(2)}) async-start(f32[64,8,8,128]{3,2,1,0:T(8,128)} %bitcast.53), calls=%async_computation.2 | async-start | bytes 4194304 | tf_op jit(solution)/shard_map/all_to_all | solution.py:55
  218.1 12.5 %all-to-all-start.6 = ((f32[8,1,769]{2,1,0:T(1,128)}), f32[8,1,769]{2,1,0:T(1,128)S(1)}, u32[]{:S(2)}, u32[]{:S(2)}) async-start(f32[8,1,769]{2,1,0:T(1,128)} %broadcast_in_dim.37), calls=%async_computation.6 | async-start | bytes 57344 | tf_op jit(solution)/shard_map/all_to_all | solution.py:14
  230.7 10.1 %all-to-all-start.3 = ((f32[8,8,128]{2,1,0:T(8,128)}), f32[8,8,128]{2,1,0:T(8,128)S(1)}, u32[]{:S(2)}, u32[]{:S(2)}) async-start(f32[8,8,128]{2,1,0:T(8,128)} %reduce_sum.65), calls=%async_computation.3 | async-start | bytes 65536 | tf_op jit(solution)/shard_map/all_to_all | solution.py:63
  242.2 54.0 %all-to-all-start.7 = ((f32[64,8,769]{2,1,0:T(8,128)}), f32[64,8,769]{2,1,0:T(8,128)}, u32[]{:S(2)}, u32[]{:S(2)}) async-start(f32[64,8,769]{2,1,0:T(8,128)} %broadcast_in_dim.38), calls=%async_computation.7 | async-start | bytes 3670016 | tf_op jit(solution)/shard_map/all_to_all | solution.py:14
  300.3 1.4 slice-start
where the time goes:
time: 309 us; the launch traced here: 307 us
  waiting for transfers between devices  171 us (55%)
  starting transfers between devices  58.9 us (19%)
  local copies, waits for them, and re-layouts  42.2 us (14%)
  blocking collectives  14 us (5%)
  matrix products  11 us (4%)
  other arithmetic  6.15 us (2%)
  between operations  3.36 us (1%)
    all_to_all x2, waiting for transfers between devices, summed_on_arrival(): lax.all_to_all(pieces, axis, split_axis=0, concat_axis=0, tiled=True)  95.5 us
    all_to_all x3, waiting for transfers between devices, from_everyone(): return lax.all_to_all(copies, axis, split_axis=0, concat_axis=0, tiled=True)  68.7 us
    all_to_all x3, starting transfers between devices, from_everyone(): return lax.all_to_all(copies, axis, split_axis=0, concat_axis=0, tiled=True)  29.8 us
    all_to_all x2, starting transfers between devices, summed_on_arrival(): lax.all_to_all(pieces, axis, split_axis=0, concat_axis=0, tiled=True)  17 us
    all_to_all x1, blocking collectives, from_everyone(): return lax.all_to_all(copies, axis, split_axis=0, concat_axis=0, tiled=True)  14 us
    concatenate x1, local copies, waits for them, and re-layouts, filled_up(): jnp.concatenate([lines, jnp.zeros((spare, *lines.shape[1:]), lines.dtype)])  13.9 us
    another operation x2, local copies, waits for them, and re-layouts, cut_along(): x.reshape(*dims[:dim], devices, dims[dim] // devices, *dims[dim + 1:])  7.4 us
    all_to_all x2, waiting for transfers between devices, sum_in_two_steps(): lax.all_to_all(nearer, far, split_axis=0, concat_axis=0, tiled=True)  6.86 us
  transfers between devices with their start and end apart: 9, of which 7 were waited for; matrix products, arithmetic and copies ran while one was open for 5% of the time, Pallas kernels for 0%

commit v1 on v0

v1 whole, which is shorter than its diff:
```python
import functools

import jax
import jax.numpy as jnp
from jax import lax
from jax.experimental import pallas as pl
from jax.experimental.pallas import tpu as pltpu
from jax.sharding import Mesh
from jax.sharding import PartitionSpec as P

SEQ = ("seq_0", "seq_1")
SEQ_DOC = ("seq_0", "seq_1", "doc_0", "doc_1")
DOC = ("doc_0", "doc_1")
MESH_ID = pl.DeviceIdType.MESH
BF = jnp.bfloat16
F32 = jnp.float32


def dot(a, b):
    return jnp.dot(a, b, preferred_element_type=F32)


def near_first(n):
    return sorted(range(1, n), key=lambda k: (min(k, n - k), k))


def kernel(
    sizes,
    t_hbm, s_hbm, a_hbm, w_hbm, first_hbm, len_hbm,
    sg_hbm, ag_ref, ug_ref, loss_ref,
    A, T, TT, S, ST, W, WT, OGT, SG, FIRST, LEN, K, KS, KR,
    UPb, UCr, UXs, UXr, UT32, UZs, UZr, UYr, UGr,
    APb, ACr, AXs, AXr, AT32, AYs, AYr, AZs, AZr,
    LC, LZ, LY, LX,
    load_sem, out_sem,
    zc_s, zc_r, gy_s, gy_r, gx_s, gx_r, gc_s, gc_r,
    h_s, h_r, k_s, k_r,
    uc_s, uc_r, ux_s, ux_r, uz_s, uz_r, uy_s, uy_r, ug_s, ug_r,
    ac_s, ac_r, ax_s, ax_r, ay_s, ay_r, az_s, az_r,
    lc_s, lc_r, lz_s, lz_r, ly_s, ly_r, lx_s, lx_r,
):
    Y, X, Z, C, td, sd, tok, scale, grad_scale, loss_scale = sizes
    y = lax.axis_index("seq_0")
    x = lax.axis_index("seq_1")
    z = lax.axis_index("doc_0")
    c = lax.axis_index("doc_1")
    half = tok // 2
    blk = td // (Y * X)
    cut = blk // C
    xr = sd // (Z * C) // X
    yx = y * X + x

    def turn(v, k, n):
        return lax.rem(v + k, n) if k else v

    def dev(dy=0, dx=0, dz=0, dc=0):
        return (turn(y, dy, Y), turn(x, dx, X), turn(z, dz, Z), turn(c, dc, C))

    def beside(step):
        s = lax.rem(yx + step, Y * X)
        return (lax.div(s, X), lax.rem(s, X), z, c)

    right = beside(1)
    left = beside(Y * X - 1)
    sends = []

    def rcopy(src, dst, ss, rs, to):
        return pltpu.make_async_remote_copy(
            src_ref=src, dst_ref=dst, send_sem=ss, recv_sem=rs, device_id=to, device_id_type=MESH_ID
        )

    def send(src, dst, ss, rs, to):
        cp = rcopy(src, dst, ss, rs, to)
        cp.start()
        sends.append(cp)

    def arrived(dst, ss, rs, to):
        rcopy(dst, dst, ss, rs, to).wait_recv()

    zc_off = [(kz, kc) for kz in range(Z) for kc in range(C) if kz or kc]
    zc_off.sort(key=lambda k: (min(k[0], Z - k[0]), k))
    y_off, x_off, z_off = near_first(Y), near_first(X), near_first(Z)

    barrier = pltpu.get_barrier_semaphore()
    peers = [dev(dz=kz, dc=kc) for kz, kc in zc_off] + [dev(dy=k) for k in y_off]
    peers += [dev(dx=k) for k in x_off] + [left, right]
    for p in peers:
        pl.semaphore_signal(barrier, inc=1, device_id=p, device_id_type=MESH_ID)

    def own_rows(zz, cc):
        return pl.ds(pl.multiple_of((zz * C + cc) * 8, 8), 8)

    loads = [
        pltpu.make_async_copy(a_hbm, A.at[yx, own_rows(z, c)], load_sem.at[0]),
        pltpu.make_async_copy(s_hbm, S, load_sem.at[1]),
        pltpu.make_async_copy(w_hbm, W, load_sem.at[2]),
        pltpu.make_async_copy(t_hbm, T, load_sem.at[3]),
        pltpu.make_async_copy(first_hbm, FIRST, load_sem.at[4]),
        pltpu.make_async_copy(len_hbm, LEN, load_sem.at[5]),
    ]
    for cp in loads:
        cp.start()

    loads[1].wait()
    loads[2].wait()
    fb = 128
    for i in range(sd // fb):
        ST[i * fb:(i + 1) * fb, :] = S[:, i * fb:(i + 1) * fb].T
    query_t = dot(W[...], ST[...]).astype(BF)
    query = query_t.T
    loads[0].wait()
    pl.semaphore_wait(barrier, len(peers))

    mine = A.at[yx, own_rows(z, c)]
    for j, (kz, kc) in enumerate(zc_off):
        send(mine, mine, zc_s.at[j], zc_r.at[j], dev(dz=kz, dc=kc))
    for i in range(sd // fb):
        WT[i * fb:(i + 1) * fb, :] = W[:, i * fb:(i + 1) * fb].T
    loads[3].wait()
    for j, (kz, kc) in enumerate(zc_off):
        zz, cc = turn(z, Z - kz if kz else 0, Z), turn(c, C - kc if kc else 0, C)
        arrived(A.at[yx, own_rows(zz, cc)], zc_s.at[j], zc_r.at[j], dev())

    def part(yy, xx):
        return A.at[yy * X + xx, pl.ds(pl.multiple_of(c * cut, cut), cut)]

    def other_part(yy, xx):
        return A.at[yy * X + xx, pl.ds(pl.multiple_of((C - 1 - c) * cut, cut), cut)]

    for k in y_off:
        send(part(y, x), part(y, x), gy_s.at[k], gy_r.at[k], dev(dy=k))
    for m in x_off:
        send(part(y, x), part(y, x), gx_s.at[m], gx_r.at[m], dev(dx=m))
    nyx = td // fb
    for i in range(Y):
        for j in range(X):
            b = i * X + j
            TT[j, i] = T[:, b * blk:(b + 1) * blk].T
    for k in y_off:
        yy = turn(y, Y - k, Y)
        arrived(part(yy, x), gy_s.at[k], gy_r.at[k], dev())
        for m in x_off:
            send(part(yy, x), part(yy, x), gx_s.at[k * X + m], gx_r.at[k * X + m], dev(dx=m))
        send(part(yy, x), part(yy, x), gc_s.at[k * X], gc_r.at[k * X], dev(dc=1))
    for k in [0] + y_off:
        yy = turn(y, Y - k if k else 0, Y)
        for m in x_off:
            xx = turn(x, X - m, X)
            arrived(part(yy, xx), gx_s.at[k * X + m], gx_r.at[k * X + m], dev())
            send(part(yy, xx), part(yy, xx), gc_s.at[k * X + m], gc_r.at[k * X + m], dev(dc=1))
    for k in [0] + y_off:
        yy = turn(y, Y - k if k else 0, Y)
        for m in [0] + x_off:
            if k or m:
                xx = turn(x, X - m if m else 0, X)
                arrived(other_part(yy, xx), gc_s.at[k * X + m], gc_r.at[k * X + m], dev())

    K[half:half + tok, :] = dot(T[...], A[...].reshape(td, 128)).astype(BF)
    send(K.at[half:tok], K.at[half + tok:2 * tok], h_s.at[0], h_r.at[0], left)
    send(K.at[tok:half + tok], K.at[0:half], h_s.at[1], h_r.at[1], right)
    loads[4].wait()
    loads[5].wait()
    first = FIRST[...]
    past = first + LEN[...]
    position = yx * tok - half + lax.broadcasted_iota(jnp.int32, (2 * tok, tok), 0)
    inside = (position >= first) & (position < past)
    arrived(K.at[half + tok:2 * tok], h_s.at[0], h_r.at[0], left)
    arrived(K.at[0:half], h_s.at[1], h_r.at[1], right)

    keys = K[...]
    keys_t = keys.T
    scores = jnp.where(inside, dot(keys, query_t) * scale, -1e30)
    top = jnp.max(scores, axis=0, keepdims=True)
    weights = jnp.where(inside, jnp.exp(scores - top), 0.0)
    prob = weights / jnp.sum(weights, axis=0, keepdims=True)
    prob_b = prob.astype(BF)
    context_t = dot(keys_t, prob_b).astype(BF)
    loss_tile = jnp.zeros((8, tok), F32)
    ctx_grad_f = jnp.zeros((128, tok), F32)
    rb = 256
    for i in range(sd // rb):
        rows = slice(i * rb, (i + 1) * rb)
        res = ST[rows, :].astype(F32) - dot(WT[rows, :], context_t)
        loss_tile = loss_tile + jnp.sum((res * res).reshape(rb // 8, 8, tok), axis=0)
        og = (-res).astype(BF)
        OGT[rows, :] = og
        ctx_grad_f = ctx_grad_f + dot(W[:, rows], og)
    ctx_grad_t = ctx_grad_f.astype(BF)
    prob_grad = dot(keys, ctx_grad_t)
    centred = prob_grad - jnp.sum(prob * prob_grad, axis=0, keepdims=True)
    score_grad = (prob * centred * scale).astype(BF)
    KS[...] = (dot(prob_b, ctx_grad_t.T) + dot(score_grad, query)).astype(BF)
    send(KS.at[0:half], KR.at[half:tok], k_s.at[0], k_r.at[0], left)
    send(KS.at[half + tok:2 * tok], KR.at[0:half], k_s.at[1], k_r.at[1], right)
    query_grad = dot(keys_t, score_grad).astype(BF).T
    context = context_t.T

    for zi in range(Z):
        for ci in range(C):
            r0 = (zi * C + ci) * xr * X
            rows = slice(r0, r0 + xr * X)
            u = (dot(OGT[rows, :], context) + dot(ST[rows, :], query_grad)).astype(BF)
            for xi in range(X):
                UPb[ci, xi, zi] = u[xi * xr:(xi + 1) * xr, :]
    far_first = list(reversed(x_off))
    for k in far_first + [0]:
        xx = turn(x, k, X)
        send(UPb.at[C - 1 - c, xx], UCr.at[xx], uc_s.at[k], uc_r.at[k], dev(dc=1))
    LC[c] = loss_tile
    send(LC.at[c], LC.at[c], lc_s.at[0], lc_r.at[0], dev(dc=1))

    arrived(KR.at[half:tok], k_s.at[0], k_r.at[0], left)
    arrived(KR.at[0:half], k_s.at[1], k_r.at[1], right)
    pair = jnp.concatenate([KS[half:half + tok, :], KR[...]], axis=1)

    def adapter_terms(k):
        xx = turn(x, k, X)
        for i in range(Y):
            two = dot(TT[xx, i], pair)
            p = (two[:, :128] + two[:, 128:]).reshape(Z, C, 8, 128)
            for ci in range(C):
                APb[ci, xx, i] = p[:, ci].reshape(cut, 128).astype(BF)
        send(APb.at[C - 1 - c, xx], ACr.at[xx], ac_s.at[k], ac_r.at[k], dev(dc=1))

    def up_core_sum(k):
        xx = turn(x, k, X)
        arrived(UCr.at[xx], uc_s.at[k], uc_r.at[k], dev())
        return UPb[c, xx].astype(F32) + UCr[xx].astype(F32)

    def adapter_core_sum(k):
        xx = turn(x, k, X)
        arrived(ACr.at[xx], ac_s.at[k], ac_r.at[k], dev())
        return APb[c, xx].astype(F32) + ACr[xx].astype(F32)

    for k in far_first:
        UXs[k - 1] = up_core_sum(k).astype(BF)
        send(UXs.at[k - 1], UXr.at[k - 1], ux_s.at[k], ux_r.at[k], dev(dx=k))
        adapter_terms(k)
    adapter_terms(0)
    for k in far_first:
        AXs[k - 1] = adapter_core_sum(k).astype(BF)
        send(AXs.at[k - 1], AXr.at[k - 1], ax_s.at[k], ax_r.at[k], dev(dx=k))

    arrived(LC.at[C - 1 - c], lc_s.at[0], lc_r.at[0], dev())
    LZ[z] = jnp.sum(LC[...], axis=0)
    for k in z_off:
        send(LZ.at[z], LZ.at[z], lz_s.at[k], lz_r.at[k], dev(dz=k))

    for i in range(sd // rb):
        cols = slice(i * rb, (i + 1) * rb)
        wc = W[:, cols]
        res = S[:, cols].astype(F32) - dot(context, wc)
        SG[:, cols] = (res + dot(query_grad, wc)).astype(BF)
    sg_out = pltpu.make_async_copy(SG, sg_hbm, out_sem.at[0])
    sg_out.start()

    total = up_core_sum(0)
    for k in x_off:
        arrived(UXr.at[k - 1], ux_s.at[k], ux_r.at[k], dev())
        total = total + UXr[k - 1].astype(F32)
    UT32[...] = total
    UZs[...] = total.astype(BF)
    for k in z_off:
        send(UZs.at[turn(z, k, Z)], UZr.at[k - 1], uz_s.at[k], uz_r.at[k], dev(dz=k))
    total = adapter_core_sum(0)
    for k in x_off:
        arrived(AXr.at[k - 1], ax_s.at[k], ax_r.at[k], dev())
        total = total + AXr[k - 1].astype(F32)
    AT32[...] = total
    AYs[...] = total.astype(BF)
    for k in y_off:
        send(AYs.at[turn(y, k, Y)], AYr.at[k - 1], ay_s.at[k], ay_r.at[k], dev(dy=k))

    for k in z_off:
        arrived(LZ.at[turn(z, Z - k, Z)], lz_s.at[k], lz_r.at[k], dev())
    LY[y] = jnp.sum(LZ[...], axis=0)
    for k in y_off:
        send(LY.at[y], LY.at[y], ly_s.at[k], ly_r.at[k], dev(dy=k))

    total = UT32[z]
    for k in z_off:
        arrived(UZr.at[k - 1], uz_s.at[k], uz_r.at[k], dev())
        total = total + UZr[k - 1].astype(F32)
    UYr[y] = total.astype(BF)
    for k in y_off:
        send(UYr.at[y], UYr.at[y], uy_s.at[k], uy_r.at[k], dev(dy=k))
    total = AT32[y]
    for k in y_off:
        arrived(AYr.at[k - 1], ay_s.at[k], ay_r.at[k], dev())
        total = total + AYr[k - 1].astype(F32)
    AZs[...] = total.reshape(Z, 8, 128)
    for k in z_off:
        send(AZs.at[turn(z, k, Z)], AZr.at[k - 1], az_s.at[k], az_r.at[k], dev(dz=k))

    for k in y_off:
        arrived(LY.at[turn(y, Y - k, Y)], ly_s.at[k], ly_r.at[k], dev())
    LX[x] = jnp.sum(LY[...], axis=0)
    for k in x_off:
        send(LX.at[x], LX.at[x], lx_s.at[k], lx_r.at[k], dev(dx=k))

    for k in y_off:
        arrived(UYr.at[turn(y, Y - k, Y)], uy_s.at[k], uy_r.at[k], dev())
    UGr[x] = jnp.sum(UYr[...].astype(F32), axis=0) * grad_scale
    for k in x_off:
        send(UGr.at[x], UGr.at[x], ug_s.at[k], ug_r.at[k], dev(dx=k))
    total = AZs[z]
    for k in z_off:
        arrived(AZr.at[k - 1], az_s.at[k], az_r.at[k], dev())
        total = total + AZr[k - 1]
    ag_ref[...] = total * grad_scale
    for k in x_off:
        arrived(LX.at[turn(x, X - k, X)], lx_s.at[k], lx_r.at[k], dev())
    all_loss = jnp.sum(LX[...], axis=0)
    loss_ref[...] = jnp.sum(jnp.sum(all_loss, axis=0, keepdims=True), axis=1, keepdims=True) * loss_scale
    for k in x_off:
        arrived(UGr.at[turn(x, X - k, X)], ug_s.at[k], ug_r.at[k], dev())
    ug_ref[...] = UGr[...].reshape(xr * X, 128).T
    for cp in sends:
        cp.wait_send()
    sg_out.wait()


def on_device(shape, teacher, student, adapter, up_weight, band_start, band_len):
    Y, X, Z, C = shape
    _, tok, td = teacher.shape
    sd, rank = student.shape[2], adapter.shape[1]
    tokens = Y * X * Z * C * tok
    sizes = (Y, X, Z, C, td, sd, tok, sd ** (-0.5), tokens ** (-0.5), 0.5 / (tokens * sd))
    blk = td // (Y * X)
    cut = blk // C
    rw = sd // (Z * C)
    xr = rw // X
    V, D = pltpu.VMEM, pltpu.SemaphoreType.DMA
    buffers = [
        V((Y * X, blk, rank), BF), V((tok, td), BF), V((X, Y, blk, tok), BF),
        V((tok, sd), BF), V((sd, tok), BF), V((rank, sd), BF), V((sd, rank), BF), V((sd, tok), BF),
        V((tok, sd), BF), V((1, tok), jnp.int32), V((1, tok), jnp.int32),
        V((2 * tok, rank), BF), V((2 * tok, rank), BF), V((tok, rank), BF),
        V((C, X, Z, xr, rank), BF), V((X, Z, xr, rank), BF), V((X - 1, Z, xr, rank), BF),
        V((X - 1, Z, xr, rank), BF), V((Z, xr, rank), F32), V((Z, xr, rank), BF),
        V((Z - 1, xr, rank), BF), V((Y, xr, rank), BF), V((X, xr, rank), F32),
        V((C, X, Y, cut, rank), BF), V((X, Y, cut, rank), BF), V((X - 1, Y, cut, rank), BF),
        V((X - 1, Y, cut, rank), BF), V((Y, cut, rank), F32), V((Y, cut, rank), BF),
        V((Y - 1, cut, rank), BF), V((Z, 8, rank), F32), V((Z - 1, 8, rank), F32),
        V((C, 8, tok), F32), V((Z, 8, tok), F32), V((Y, 8, tok), F32), V((X, 8, tok), F32),
    ]
    counts = [Z * C, Y, Y * X, Y * X, 2, 2, X, X, Z, Y, X, X, X, Y, Z, 1, Z, Y, X]
    sems = [D((6,)), D((1,))]
    for n in counts:
        sems += [D((n,)), D((n,))]
    any_spec = pl.BlockSpec(memory_space=pl.ANY)
    vmem = pl.BlockSpec(memory_space=pltpu.VMEM)
    sg, ag, ug, loss = pl.pallas_call(
        functools.partial(kernel, sizes),
        out_shape=(
            jax.ShapeDtypeStruct((tok, sd), BF),
            jax.ShapeDtypeStruct((8, rank), F32),
            jax.ShapeDtypeStruct((rank, rw), F32),
            jax.ShapeDtypeStruct((1, 1), F32),
        ),
        in_specs=[any_spec] * 6,
        out_specs=(any_spec, vmem, vmem, vmem),
        scratch_shapes=buffers + sems,
        compiler_params=pltpu.CompilerParams(
            collective_id=0, has_side_effects=True, vmem_limit_bytes=60 * 2**20
        ),
    )(teacher[0], student[0], adapter, up_weight, band_start, band_len)
    return sg[None], ag, ug, loss[0, 0]


def build(torus):
    shape = tuple(torus.shape[a] for a in SEQ_DOC)
    placed = (P(DOC, SEQ, None), P(DOC, SEQ, None), P(SEQ_DOC, None), P(), P(DOC, SEQ), P(DOC, SEQ))
    return jax.shard_map(
        functools.partial(on_device, shape),
        mesh=torus,
        in_specs=placed,
        out_specs=(P(DOC, SEQ, None), P(SEQ_DOC, None), P(None, DOC), P()),
        check_vma=False,
    )


def solution(mesh):
    return build(Mesh(mesh.devices.reshape(8, 4, 8, 2), SEQ_DOC))
```

time: 309 us -> 73.9 us (0.24)
  waiting for transfers between devices: 171 us -> 0 us
  Pallas kernels: 0 us -> 66.6 us
  starting transfers between devices: 58.9 us -> 0 us
  local copies, waits for them, and re-layouts: 42.2 us -> 4.3 us
  blocking collectives: 14 us -> 0 us
  matrix products: 11 us -> 0 us
  other arithmetic: 6.15 us -> 0 us
    all_to_all x7 -> x0, waiting for transfers between devices: 171 us -> none  [the longest x2 95.5 us: summed_on_arrival(): lax.all_to_all(pieces, axis, split_axis=0, concat_axis=0, tiled=True)]
    pallas_call x0 -> x1, Pallas kernels: none -> 66.6 us  [on_device(): pl.pallas_call(functools.partial(kernel, sizes), out_shape=(jax.ShapeDtyp...]
    all_to_all x7 -> x0, starting transfers between devices: 53.5 us -> none  [the longest x3 29.8 us: from_everyone(): return lax.all_to_all(copies, axis, split_axis=0, concat_axis=0, tiled=True)]
    all_to_all x1 -> x0, blocking collectives: 14 us -> none  [from_everyone(): return lax.all_to_all(copies, axis, split_axis=0, concat_axis=0, tiled=True)]
    concatenate x1 -> x0, local copies, waits for them, and re-layouts: 13.9 us -> none  [filled_up(): jnp.concatenate([lines, jnp.zeros((spare, *lines.shape[1:]), lines.dtype)])]
    dot_general x13 -> x0, matrix products: 11 us -> none  [the longest x4 5.12 us: contract_rows(): lax.dot_general(left, right, (((0,), (0,)), ((), ())), preferred_element_...]
    another operation x3 -> x0, local copies, waits for them, and re-layouts: 9.73 us -> none  [the longest x2 7.4 us: cut_along(): x.reshape(*dims[:dim], devices, dims[dim] // devices, *dims[dim + 1:])]
    transpose x2 -> x0, local copies, waits for them, and re-layouts: 5.65 us -> none  [the longest x1 3.8 us: cut_along(): return jnp.moveaxis(pieces, dim, 0)]
  transfers between devices with their start and end apart: 9 -> 0, of which waited for: 7 -> 0; matrix products, arithmetic and copies ran while one was open for 5% -> 0% of each run, Pallas kernels for 0% -> 0%
where the time goes in v1:
time: 73.9 us; the launch traced here: 73.3 us
  Pallas kernels  66.6 us (90%)
  local copies, waits for them, and re-layouts  4.3 us (6%)
  between operations  2.41 us (3%)
    pallas_call x1, Pallas kernels, on_device(): pl.pallas_call(functools.partial(kernel, sizes), out_shape=(jax.ShapeDtyp...  66.6 us
    unnamed x5, local copies, waits for them, and re-layouts  4.3 us

profile of v1, /device:TPU:1, one launch (start us, length us, event | category | flops | bytes accessed | tf_op | source)
XLA Modules:
  0.0 73.3 jit_solution(11482844070316338704)
XLA Ops:
  0.6 66.6 %shard_map.93 = (bf16[128,3072]{1,0:T(8,128)(2,1)}, f32[8,128]{1,0:T(8,128)}, f32[128,192]{1,0:T(8,128)}, f32[1,1]{1,0:T(1,128)}) custom-call(bf16[128,4096]{1,0:T(8,128)(2,1)} %bitcast.4, bf16[128,3072]{1,0:T(8,128)(2,1)} %bitcast.6, bf16[8,128]{1,0:T(8,128)(2,1)} %a_hbm.1, bf16[128,3072]{1,0:T(8,128)(2,1)} %w_hbm.1, s32[1,128]{1,0:T(1,128)} %first_hbm.1, ...), custom_call_target="tpu_custom_call" | custom-call | tf_op jit(solution)/shard_map/pallas_call | solution.py:353
  67.2 1.6 %copy.10 = f32[128,192]{0,1:T(8,128)} copy(f32[128,192]{1,0:T(8,128)} %get-tuple-element.14) | data formatting | bytes 196608
  68.9 0.0 copy-start
  68.9 2.1 %copy.14 = bf16[1,128,3072]{2,1,0:T(8,128)(2,1)} copy(bf16[1,128,3072]{2,1,0:T(8,128)(2,1)} %bitcast.5) | data formatting | bytes 1572864
  71.0 0.0 copy-done
  71.0 0.6 copy.15
Async XLA Ops:
  68.9 2.1 %copy-start = (f32[8,128]{1,0:T(8,128)S(1)}, f32[8,128]{1,0:T(8,128)}, u32[]{:S(2)}) copy-start(f32[8,128]{1,0:T(8,128)} %get-tuple-element.21) | copy-start | bytes 12292
